TPU v7x, 32 devices: a whole 2x2x4 slice. The times are simulated.
32 devices in a mesh: grp: 1, dev: 32 (over z, y, x, core).
Axes of the slice: x: 2, y: 2, z: 4, core: 2. Of those that a mesh axis runs over, the one named last changes fastest.
Arguments:
- hidden_in: bfloat16 [640, 32, 768], P(('grp', 'dev')), may hold values from -6 to 6
- grad_out: bfloat16 [640, 32, 768], P(('grp', 'dev')), may hold values from -6 to 6
- norm_gain: float32 [768], replicated, may hold values from 0.25 to 1.75
- w_qkv: bfloat16 [768, 2304], replicated, may hold values from -0.21875 to 0.21875
- w_out: bfloat16 [768, 768], replicated, may hold values from -0.21875 to 0.21875
- sharpness: float32 [12], replicated, may hold values from 4 to 20
- cohort_ids: int32 [640], P('grp'), may hold values from 0 to 3
- observed: int32 [640, 32], P('grp', 'dev'), may hold values 0 or 1
Outputs:
- grad_in: bfloat16 [640, 32, 768], P(('grp', 'dev'))
- grad_qkv: float32 [768, 2304], P(('grp', 'dev'))
- grad_wout: float32 [768, 768], P(('grp', 'dev'))
All inputs are finite; a program needn't handle non-finite values. No bound on the sum of `observed` on one device may be relied on, other than what follows from the above.
Results may differ from a plain program's by a relative error of at most 0.015.
Values may be sent and summed in bfloat16 or wider, within the bound.
A program may use at most 128 MiB of HBM per device.

v0:
```python
import functools
import math

import jax
import jax.numpy as jnp
from jax import lax
from jax.experimental import pallas as pl
from jax.experimental.pallas import tpu as pltpu
from jax.sharding import PartitionSpec as P

epsilon = 1e-06
log2e = math.log2(math.e)
cohort_kinds = 4


def dot(left, right, dims):
    return lax.dot_general(left, right, ((dims[0], dims[1]), ((), ())), preferred_element_type=jnp.float32)


def forward_kernel(
    head_size,
    group,
    sharp_ref,
    x_ref,
    gain_ref,
    wq_ref,
    wk_ref,
    wv_ref,
    cohort_col_ref,
    cohort_row_ref,
    seen_ref,
    normed_t_ref,
    q_ref,
    k_ref,
    k_t_ref,
    v_ref,
    inv_ref,
    probs_ref,
    att_ref,
    normed_ref,
    mask_ref,
):
    step = pl.program_id(0)
    rows, width = x_ref.shape

    @pl.when(step == 0)
    def _():
        values = x_ref[...].astype(jnp.float32)
        inv = lax.rsqrt(jnp.mean(values * values, axis=-1, keepdims=True) + epsilon)
        normed = values * inv * gain_ref[...]
        normed_ref[...] = normed.astype(jnp.bfloat16)
        normed_t_ref[...] = normed.T.astype(jnp.bfloat16)
        same = cohort_col_ref[...] == cohort_row_ref[...]
        diagonal = lax.broadcasted_iota(jnp.int32, (rows, rows), 0) == lax.broadcasted_iota(
            jnp.int32, (rows, rows), 1
        )
        seen = jnp.broadcast_to(seen_ref[...], (rows, rows)) == 1
        mask_ref[...] = jnp.where(same & (seen | diagonal), 1.0, 0.0)

    normed = normed_ref[...]
    q_raw = dot(normed, wq_ref[...], ((1,), (0,)))
    k_raw = dot(normed, wk_ref[...], ((1,), (0,)))
    v_raw = dot(normed, wv_ref[...], ((1,), (0,)))
    v_ref[...] = v_raw.astype(jnp.bfloat16)
    for h in range(group):
        base = h * head_size
        lanes = slice(base, base + head_size)
        q = q_raw[:, lanes]
        k = k_raw[:, lanes]
        v_t = v_raw[:, lanes].T.astype(jnp.bfloat16)
        q_inv = lax.rsqrt(jnp.mean(q * q, axis=-1, keepdims=True) + epsilon)
        k_inv = lax.rsqrt(jnp.mean(k * k, axis=-1, keepdims=True) + epsilon)
        q_half = (q * q_inv).astype(jnp.bfloat16)
        k_unit = k * k_inv
        k_half = k_unit.astype(jnp.bfloat16)
        k_t_ref[lanes, :] = k_unit.T.astype(jnp.bfloat16)
        q_ref[:, lanes] = q_half
        k_ref[:, lanes] = k_half
        inv_ref[0, :, h : h + 1] = q_inv
        inv_ref[0, :, group + h : group + h + 1] = k_inv
        scale = sharp_ref[step * group + h] / head_size
        scores = dot(k_half, q_half, ((1,), (1,)))
        weights = jnp.exp2(scores * (scale * log2e)) * mask_ref[...]
        probs = weights * (1.0 / jnp.sum(weights, axis=0, keepdims=True))
        probs_half = probs.astype(jnp.bfloat16)
        probs_ref[h] = probs_half
        att_ref[base : base + head_size, :] = dot(v_t, probs_half, ((1,), (0,))).astype(jnp.bfloat16)


def backward_kernel(
    head_size,
    group,
    sharp_ref,
    x_ref,
    dy_ref,
    gain_ref,
    wqkv_t_ref,
    wo_t_ref,
    q_ref,
    k_ref,
    k_t_ref,
    v_ref,
    inv_ref,
    probs_ref,
    gin_ref,
    dproj_ref,
):
    step = pl.program_id(0)
    gw = group * head_size
    width = x_ref.shape[1]
    da_half = dot(dy_ref[...], wo_t_ref[...], ((1,), (0,))).astype(jnp.bfloat16)
    parts = ([], [], [])
    for h in range(group):
        base = h * head_size
        lanes = slice(base, base + head_size)
        q_half = q_ref[:, lanes]
        q_unit = q_half.astype(jnp.float32)
        k_unit = k_ref[:, lanes].astype(jnp.float32)
        da = da_half[:, lanes]
        q_inv = inv_ref[0, :, h : h + 1]
        k_inv = inv_ref[0, :, group + h : group + h + 1]
        scale = sharp_ref[step * group + h] / head_size
        grad_probs = dot(v_ref[:, lanes], da, ((1,), (1,)))
        probs_half = probs_ref[h]
        probs = probs_half.astype(jnp.float32)
        grad_v = dot(probs_half, da, ((1,), (0,)))
        row_dot = jnp.sum(grad_probs * probs, axis=0, keepdims=True)
        grad_scores = (probs * (grad_probs - row_dot)).astype(jnp.bfloat16)
        dq = dot(k_t_ref[lanes, :], grad_scores, ((1,), (0,))).T * scale
        dk = dot(grad_scores, q_half, ((1,), (0,))) * scale
        dq = q_inv * (dq - q_unit * jnp.mean(dq * q_unit, axis=-1, keepdims=True))
        dk = k_inv * (dk - k_unit * jnp.mean(dk * k_unit, axis=-1, keepdims=True))
        for part, value in zip(parts, (dq, dk, grad_v)):
            part.append(value.astype(jnp.bfloat16))
    for at, part in enumerate(parts):
        start = pl.multiple_of(at * width + step * gw, gw)
        dproj_ref[:, pl.ds(start, gw)] = jnp.concatenate(part, axis=1)

    @pl.when(step == pl.num_programs(0) - 1)
    def _():
        values = x_ref[...].astype(jnp.float32)
        inv = lax.rsqrt(jnp.mean(values * values, axis=-1, keepdims=True) + epsilon)
        unit = values * inv
        shaped = dot(dproj_ref[...], wqkv_t_ref[...], ((1,), (0,))) * gain_ref[...]
        result = dy_ref[...].astype(jnp.float32) + inv * (
            shaped - unit * jnp.mean(shaped * unit, axis=-1, keepdims=True)
        )
        gin_ref[...] = result.astype(jnp.bfloat16)


def weights_kernel(normed_t_ref, att_ref, dq_ref, dk_ref, dv_ref, dy_ref, gqkv_ref, gwo_ref):
    dproj = jnp.concatenate([dq_ref[...], dk_ref[...], dv_ref[...]], axis=1)
    gqkv_ref[0] = dot(normed_t_ref[...], dproj, ((1,), (0,))).astype(jnp.bfloat16)
    gwo_ref[...] = dot(att_ref[...], dy_ref[...], ((1,), (0,))).astype(jnp.bfloat16)


def patch_grads(x, dy, norm_gain, w_qkv, w_out, sharpness, cohort_ids, seen):
    rows, width = x.shape
    heads = sharpness.shape[0]
    head_size = width // heads
    group = math.gcd(heads, 2)
    steps = heads // group
    gw = group * head_size
    half = jnp.bfloat16
    whole = lambda shape: pl.BlockSpec(shape, lambda g: (0,) * len(shape))
    cols = lambda n: pl.BlockSpec((rows, n), lambda g: (0, g))
    lines = lambda n: pl.BlockSpec((gw, n), lambda g: (g, 0))
    smem = pl.BlockSpec(memory_space=pltpu.SMEM)
    weights = [
        pl.BlockSpec((width, gw), lambda g: (0, g)),
        pl.BlockSpec((width, gw), lambda g: (0, steps + g)),
        pl.BlockSpec((width, gw), lambda g: (0, 2 * steps + g)),
    ]
    invs = pl.BlockSpec((1, rows, 2 * group), lambda g: (g, 0, 0))
    probs_spec = pl.BlockSpec((group, rows, rows), lambda g: (g, 0, 0))
    w_qkv_t, w_out_t = w_qkv.T, w_out.T
    params = pltpu.CompilerParams(vmem_limit_bytes=60 * 1024 * 1024)

    def cost(flops):
        return pl.CostEstimate(flops=flops, bytes_accessed=rows * width * 20, transcendentals=0)

    forward = pl.pallas_call(
        functools.partial(forward_kernel, head_size, group),
        grid=(steps,),
        in_specs=[smem, whole((rows, width)), whole((1, width))]
        + weights
        + [whole((rows, 1)), whole((1, rows)), whole((rows, 1))],
        out_specs=[whole((width, rows)), cols(gw), cols(gw), lines(rows), cols(gw), invs, probs_spec, lines(rows)],
        out_shape=[
            jax.ShapeDtypeStruct((width, rows), half),
            jax.ShapeDtypeStruct((rows, width), half),
            jax.ShapeDtypeStruct((rows, width), half),
            jax.ShapeDtypeStruct((width, rows), half),
            jax.ShapeDtypeStruct((rows, width), half),
            jax.ShapeDtypeStruct((steps, rows, 2 * group), jnp.float32),
            jax.ShapeDtypeStruct((heads, rows, rows), half),
            jax.ShapeDtypeStruct((width, rows), half),
        ],
        scratch_shapes=[
            pltpu.VMEM((rows, width), half),
            pltpu.VMEM((rows, rows), jnp.float32),
        ],
        compiler_params=params,
        cost_estimate=cost(40_000_000_000),
    )
    with jax.named_scope("forward_part"):
        normed_t, q, k, k_t, v, inv, probs, att = forward(
            sharpness,
            x,
            norm_gain[None, :],
            w_qkv,
            w_qkv,
            w_qkv,
            cohort_ids[:, None],
            cohort_ids[None, :],
            seen,
        )
    gin, dproj = pl.pallas_call(
        functools.partial(backward_kernel, head_size, group),
        grid=(steps,),
        in_specs=[
            smem,
            whole((rows, width)),
            whole((rows, width)),
            whole((1, width)),
            whole((3 * width, width)),
            pl.BlockSpec((width, gw), lambda g: (0, g)),
            cols(gw),
            cols(gw),
            lines(rows),
            cols(gw),
            invs,
            probs_spec,
        ],
        out_specs=[whole((rows, width)), whole((rows, 3 * width))],
        out_shape=[
            jax.ShapeDtypeStruct((rows, width), half),
            jax.ShapeDtypeStruct((rows, 3 * width), half),
        ],
        compiler_params=params,
        cost_estimate=cost(25_000_000_000),
    )(sharpness, x, dy, norm_gain[None, :], w_qkv_t, w_out_t, q, k, k_t, v, inv, probs)
    gqkv, gwo = pl.pallas_call(
        weights_kernel,
        grid=(steps,),
        in_specs=[
            whole((width, rows)),
            lines(rows),
            cols(gw),
            pl.BlockSpec((rows, gw), lambda g: (0, steps + g)),
            pl.BlockSpec((rows, gw), lambda g: (0, 2 * steps + g)),
            whole((rows, width)),
        ],
        out_specs=[pl.BlockSpec((1, width, 3 * gw), lambda g: (g, 0, 0)), lines(width)],
        out_shape=[
            jax.ShapeDtypeStruct((steps, width, 3 * gw), half),
            jax.ShapeDtypeStruct((width, width), half),
        ],
        compiler_params=pltpu.CompilerParams(vmem_limit_bytes=30 * 1024 * 1024),
        cost_estimate=cost(8_000_000_000),
    )(normed_t, att, dproj, dproj, dproj, dy)
    return gin, gqkv, gwo


def scatter_kernel(n, chunks, group_cols, qkv_ref, wo_ref, out_ref, wout_ref, *scratch):
    bits = n.bit_length() - 1
    recv = scratch[:bits]
    kept = (None,) + scratch[bits : 2 * bits - 1]
    send_sem, recv_sem = scratch[2 * bits - 1 :]
    me = lax.axis_index("dev")
    bit = [(me // (1 << b)) % 2 for b in range(bits)]
    peer = [me + (1 - 2 * bit[b]) * (1 << b) for b in range(bits)]
    groups = qkv_ref.shape[0]
    cols = qkv_ref.shape[-1]
    width = wout_ref.shape[-1]

    barrier = pltpu.get_barrier_semaphore()
    for b in range(bits):
        pl.semaphore_signal(
            barrier, inc=1, device_id={"dev": peer[b]}, device_id_type=pl.DeviceIdType.MESH
        )
    pl.semaphore_wait(barrier, bits)

    def order_of(chunk):
        order = list(range(bits))
        if chunk % 2 and bits > 2:
            order[1], order[2] = order[2], order[1]
        return order

    def source(chunk, phase, side):
        order = order_of(chunk)
        left = sorted(set(range(bits)) - set(order[:phase]), reverse=True)
        picks = tuple(side if b == order[phase] else slice(None) for b in left)
        if phase:
            return kept[phase], (chunk,) + picks
        if chunk < groups:
            return qkv_ref, (chunk,) + picks
        start = (chunk - groups) * cols
        return wo_ref, picks + (slice(None), slice(start, start + cols))

    copies = {}

    def begin(chunk, phase):
        b = order_of(chunk)[phase]
        ref, index = source(chunk, phase, 1 - bit[b])
        copy = pltpu.make_async_remote_copy(
            src_ref=ref.at[index],
            dst_ref=recv[phase].at[chunk],
            send_sem=send_sem.at[chunk, phase],
            recv_sem=recv_sem.at[chunk, phase],
            device_id={"dev": peer[b]},
            device_id_type=pl.DeviceIdType.MESH,
        )
        copy.start()
        copies[chunk, phase] = copy

    def finish(chunk, phase):
        b = order_of(chunk)[phase]
        copies[chunk, phase].wait_recv()
        ref, index = source(chunk, phase, bit[b])
        total = ref[index].astype(jnp.float32) + recv[phase][chunk].astype(jnp.float32)
        if phase + 1 < bits:
            kept[phase + 1][chunk] = total.astype(jnp.bfloat16)
            begin(chunk, phase + 1)
        elif chunk < groups:
            for part in range(3):
                at = part * width + chunk * group_cols
                out_ref[:, at : at + group_cols] = total[
                    :, part * group_cols : (part + 1) * group_cols
                ]
        else:
            at = (chunk - groups) * cols
            wout_ref[:, at : at + cols] = total

    for chunk in range(chunks):
        begin(chunk, 0)
    pairs = -(-chunks // 2)
    for wave in range(pairs + bits - 1):
        for phase in reversed(range(bits)):
            pair = wave - phase
            if 0 <= pair < pairs:
                for chunk in range(2 * pair, min(2 * pair + 2, chunks)):
                    finish(chunk, phase)
    for copy in copies.values():
        copy.wait_send()


def scatter_sums(gqkv, gwo, n):
    groups, width, cols = gqkv.shape
    bits = n.bit_length() - 1
    rows = width // n
    chunks = groups + width // cols
    cube = (2,) * bits
    recv = [pltpu.VMEM((chunks,) + (2,) * (bits - 1 - p) + (rows, cols), jnp.bfloat16) for p in range(bits)]
    kept = [pltpu.VMEM((chunks,) + (2,) * (bits - p) + (rows, cols), jnp.bfloat16) for p in range(1, bits)]
    vmem = pl.BlockSpec(memory_space=pltpu.VMEM)
    return pl.pallas_call(
        functools.partial(scatter_kernel, n, chunks, cols // 3),
        in_specs=[vmem, vmem],
        out_specs=[vmem, vmem],
        out_shape=[
            jax.ShapeDtypeStruct((rows, 3 * width), jnp.float32),
            jax.ShapeDtypeStruct((rows, width), jnp.float32),
        ],
        scratch_shapes=recv
        + kept
        + [pltpu.SemaphoreType.DMA((chunks, bits)), pltpu.SemaphoreType.DMA((chunks, bits))],
        compiler_params=pltpu.CompilerParams(
            collective_id=0, has_side_effects=True, vmem_limit_bytes=40 * 1024 * 1024
        ),
        cost_estimate=pl.CostEstimate(
            flops=40_000_000_000, bytes_accessed=8 * gqkv.size, transcendentals=0
        ),
    )(gqkv.reshape((groups,) + cube + (rows, cols)), gwo.reshape(cube + (rows, width)))


def layer(n, hidden_in, grad_out, norm_gain, w_qkv, w_out, sharpness, cohort_ids, observed):
    width = hidden_in.shape[-1]
    x = lax.all_to_all(hidden_in, "dev", split_axis=1, concat_axis=0, tiled=True)
    with jax.named_scope("cotangent_move"):
        dy = lax.all_to_all(grad_out, "dev", split_axis=1, concat_axis=0, tiled=True)
    campaigns, patches, _ = x.shape
    gin, gqkv, gwo = [], 0.0, 0.0
    for p in range(patches):
        a, b, c = patch_grads(
            x[:, p], dy[:, p], norm_gain, w_qkv, w_out, sharpness, cohort_ids, observed[:, p : p + 1]
        )
        gin.append(a.reshape(n, campaigns // n, width))
        gqkv, gwo = (b, c) if p == 0 else (gqkv + b, gwo + c)
    gin = gin[0] if patches == 1 else jnp.stack(gin, axis=1).reshape(n * patches, campaigns // n, width)
    grad_in = lax.all_to_all(gin, "dev", split_axis=0, concat_axis=0, tiled=True).transpose(1, 0, 2)
    grad_qkv, grad_wout = scatter_sums(gqkv, gwo, n)
    return (grad_in, grad_qkv, grad_wout)


def steps_to(total, body):
    lax.fori_loop(0, total, lambda i, c: (body(i), c)[1], 0)


def fused_kernel(
    n,
    block,
    cohorts,
    head_size,
    sharp_ref,
    x_hbm,
    dy_hbm,
    wqkv_hbm,
    wo_hbm,
    gain_ref,
    cohort_ref,
    seen_ref,
    gin_ref,
    gqkv_ref,
    gwo_ref,
    x_in,
    dy_in,
    wqkv_ref,
    wo_ref,
    flat,
    x_out,
    dy_out,
    x_got,
    dy_got,
    gin_got,
    tail_ref,
    got_ref,
    place_ref,
    place_t_ref,
    mask_ref,
    xs_ref,
    normed_ref,
    normed_t_ref,
    q_ref,
    k_ref,
    v_ref,
    q_inv_ref,
    k_inv_ref,
    probs_ref,
    att_ref,
    dys_ref,
    da_ref,
    dproj_ref,
    sums_ref,
    *rest,
):
    bits = n.bit_length() - 1
    recv = rest[:bits]
    local_sem, send_sem, recv_sem, sum_send, sum_recv = rest[bits:]
    half, full = jnp.bfloat16, jnp.float32
    per, patches, width = x_in.shape
    campaigns = per * n
    lanes = 128
    cuts = width // lanes
    middle = width // 2
    rows = block * cohorts
    heads = width // head_size
    pair = lanes // head_size
    groups = heads // pair
    wide = pair * block
    major = per - per % 16
    minor = per % 16
    tiles = major // 8
    spread = per + 8 - per % 8
    log_heads = groups
    me = lax.axis_index("dev")

    def other(i):
        return lax.rem(me + i, n)

    def before(i):
        return lax.rem(me + n - i, n)

    loads = [
        pltpu.make_async_copy(a, b, local_sem.at[i])
        for i, (a, b) in enumerate(((x_hbm, x_in), (dy_hbm, dy_in), (wqkv_hbm, wqkv_ref), (wo_hbm, wo_ref)))
    ]
    for load in loads:
        load.start()
    barrier = pltpu.get_barrier_semaphore()

    def greet(i):
        pl.semaphore_signal(
            barrier, inc=1, device_id={"dev": other(i + 1)}, device_id_type=pl.DeviceIdType.MESH
        )

    steps_to(n - 1, greet)

    def prepare(source, out):
        def widen(c):
            start = pl.multiple_of(c * patches, 8)
            for b in range(cuts):
                flat[b, pl.ds(start, patches), :] = source[c, :, b * lanes : (b + 1) * lanes].astype(full)

        def pick(p):
            for b in range(cuts):
                to, at = divmod(b, cuts // 2)
                at = slice(at * lanes, (at + 1) * lanes)
                body = flat[b, pl.ds(p, major, stride=patches), :].reshape(tiles, 8, lanes)
                out[p, to * tiles : (to + 1) * tiles, :, at] = body.astype(half)
            ends = []
            for b in range(cuts):
                ends.append(flat[b, pl.ds(major * patches + p, minor, stride=patches), :])
            for b in range(cuts // 2):
                both = jnp.concatenate([ends[b], ends[b + cuts // 2]], axis=0)
                out[p, 2 * tiles, :, b * lanes : (b + 1) * lanes] = both.astype(half)

        steps_to(per, widen)
        steps_to(n, pick)

    def transfer(kind, out, got, to, slot):
        return pltpu.make_async_remote_copy(
            src_ref=out.at[to],
            dst_ref=got.at[slot],
            send_sem=send_sem.at[kind, to],
            recv_sem=recv_sem.at[kind, slot],
            device_id={"dev": to},
            device_id_type=pl.DeviceIdType.MESH,
        )

    def send_all(kind, out, got):
        steps_to(n - 1, lambda i: transfer(kind, out, got, other(i + 1), me).start())

    def sent_all(kind, out, got):
        steps_to(n - 1, lambda i: transfer(kind, out, got, other(i + 1), me).wait_send())

    def arrived(kind, out, got, source):
        transfer(kind, out, got, source, source).wait_recv()

    loads[0].wait()
    prepare(x_in, x_out)
    pl.semaphore_wait(barrier, n - 1)
    send_all(0, x_out, x_got)
    x_got[me] = x_out[me]
    loads[1].wait()
    prepare(dy_in, dy_out)
    dy_got[me] = dy_out[me]
    send_all(1, dy_out, dy_got)

    cohort = cohort_ref[...]
    line8 = jnp.broadcast_to(cohort.astype(full), (8, campaigns))
    column = line8.T[:, 0:1]
    same = (column == cohort.astype(full)) & (
        lax.broadcasted_iota(jnp.int32, (campaigns, campaigns), 0)
        < lax.broadcasted_iota(jnp.int32, (campaigns, campaigns), 1)
    )
    rank = jnp.sum(jnp.where(same, 1.0, 0.0), axis=0, keepdims=True)
    spot = cohort.astype(full) * block + rank
    high = jnp.floor(spot * (1 / 16))
    low = spot - 16 * high
    tags = jnp.concatenate(
        [high, low, seen_ref[...].astype(full), jnp.zeros((5, campaigns), full)], axis=0
    ).astype(half)
    slots = n * (major + 8)
    slot = lax.broadcasted_iota(jnp.int32, (1, slots), 1)
    after = slot - n * major
    in_major = slot < n * major
    first = in_major | (after % 8 < 4)
    owner = jnp.where(
        in_major, (slot // major) * per + slot % major, (after // 8) * per + major + after % minor
    )
    pick = jnp.where(lax.broadcasted_iota(jnp.int32, (campaigns, slots), 0) == owner, 1.0, 0.0)
    tags = dot(tags, pick.astype(half), ((1,), (0,)))
    spot = 16 * tags[0:1] + tags[1:2]
    spot8 = jnp.broadcast_to(spot, (8, slots))
    place = jnp.where(lax.broadcasted_iota(jnp.int32, (rows, slots), 0).astype(full) == spot, 1.0, 0.0)
    place_ref[...] = place.astype(half)
    place_t = jnp.where(lax.broadcasted_iota(jnp.int32, (slots, rows), 1).astype(full) == spot8.T[:, 0:1], 1.0, 0.0)
    place_t_ref[...] = place_t.astype(half)
    known = jnp.where(first, tags[2:3], 0.0)
    known = dot(place_ref[...], jnp.broadcast_to(known, (8, slots)).astype(half), ((1,), (1,)))[:, 0:1]
    for c in range(cohorts):
        row = lax.broadcasted_iota(jnp.int32, (block, block), 0)
        col = lax.broadcasted_iota(jnp.int32, (block, block), 1)
        mine = jnp.broadcast_to(known[c * block : (c + 1) * block], (block, block))
        square = jnp.where((row == col) | (mine > 0.5), 1.0, 0.0)
        mask_ref[c * block : (c + 1) * block, :] = jnp.concatenate([square] * pair, axis=1)

    lane = lax.broadcasted_iota(jnp.int32, (1, lanes), 1)
    ones_row = lax.broadcasted_iota(jnp.int32, (2 * lanes, lanes), 0) % lanes // head_size
    ones_col = lax.broadcasted_iota(jnp.int32, (2 * lanes, lanes), 1) // head_size
    ones = jnp.where(ones_row == ones_col, 1.0 / head_size, 0.0).astype(half)

    def head_mean(values):
        upper = values.astype(half)
        lower = (values - upper.astype(full)).astype(half)
        return dot(jnp.concatenate([upper, lower], axis=1), ones, ((1,), (0,)))

    def split(values):
        return jnp.concatenate(
            [jnp.where(lane // head_size == h, values, jnp.zeros_like(values)) for h in range(pair)], axis=0
        )

    def gather(kind, out, got):
        def take(source):
            values = got[source].astype(full)
            start = pl.multiple_of(source * major, 16)
            got_ref[pl.ds(start, major), 0:middle] = values[0:tiles].reshape(major, middle).astype(half)
            got_ref[pl.ds(start, major), middle:width] = (
                values[tiles : 2 * tiles].reshape(major, middle).astype(half)
            )
            tail_ref[pl.ds(pl.multiple_of(source * 8, 8), 8), :] = values[2 * tiles]

        def step(i):
            source = before(i + 1)
            arrived(kind, out, got, source)
            take(source)

        take(me)
        steps_to(n - 1, step)
        ends = tail_ref[...]
        upper = lax.broadcasted_iota(jnp.int32, ends.shape, 0) % 8 < 4
        start = n * major
        got_ref[start:, 0:middle] = jnp.where(upper, ends, 0.0).astype(half)
        got_ref[start:, middle:width] = jnp.where(upper, 0.0, ends).astype(half)

    loads[2].wait()
    loads[3].wait()
    gather(0, x_out, x_got)

    def settle(c):
        at = pl.ds(pl.multiple_of(c * block, block), block)
        values = dot(place_ref[at, :], got_ref[...], ((1,), (0,)))
        xs_ref[at, :] = values.astype(half)
        inv = lax.rsqrt(jnp.mean(values * values, axis=-1, keepdims=True) + epsilon)
        normed_ref[at, :] = (values * inv * gain_ref[...]).astype(half)

    steps_to(cohorts, settle)

    def turn(b):
        at = pl.ds(pl.multiple_of(b * lanes, lanes), lanes)
        normed_t_ref[at, :] = normed_ref[:, at].astype(full).T.astype(half)

    def project(g):
        def raw(part):
            at = pl.ds(pl.multiple_of(part * width + g * lanes, lanes), lanes)
            return dot(normed_ref[...], wqkv_ref[:, at], ((1,), (0,)))

        at = pl.ds(pl.multiple_of(g * lanes, lanes), lanes)
        for part, (unit_ref, inv_ref) in enumerate(((q_ref, q_inv_ref), (k_ref, k_inv_ref))):
            values = raw(part)
            inv = lax.rsqrt(head_mean(values * values) + epsilon)
            unit_ref[:, at] = (values * inv).astype(half)
            inv_ref[:, at] = inv
        v_ref[:, at] = raw(2).astype(half)

    steps_to(groups, project)
    steps_to(cuts, turn)

    def scale_of(g, axis, size):
        shape = (1, size) if axis else (size, 1)
        index = lax.broadcasted_iota(jnp.int32, shape, axis)
        scale = jnp.zeros(shape, full)
        for h in range(pair):
            scale = jnp.where(index // (size // pair) == h, sharp_ref[g * pair + h] / head_size, scale)
        return scale

    def fold(values):
        return jnp.concatenate(
            [
                values[h * head_size : (h + 1) * head_size, h * block : (h + 1) * block]
                for h in range(pair)
            ],
            axis=0,
        )

    def attend(g):
        at = pl.ds(pl.multiple_of(g * lanes, lanes), lanes)
        scale = scale_of(g, 1, wide) * log2e
        for c in range(cohorts):
            block_rows = slice(c * block, (c + 1) * block)
            scores = dot(k_ref[block_rows, at], split(q_ref[block_rows, at]), ((1,), (1,)))
            weights = jnp.exp2(scores * scale) * mask_ref[block_rows, :]
            probs = (weights * (1.0 / jnp.sum(weights, axis=0, keepdims=True))).astype(half)
            probs_ref[g * cohorts + c] = probs
            att = dot(v_ref[block_rows, at].T, probs, ((1,), (0,)))
            att_ref[c, at, :] = fold(att).astype(half)

    steps_to(groups, attend)

    gather(1, dy_out, dy_got)

    def settle_dy(c):
        at = pl.ds(pl.multiple_of(c * block, block), block)
        dys_ref[at, :] = dot(place_ref[at, :], got_ref[...], ((1,), (0,))).astype(half)

    steps_to(cohorts, settle_dy)

    bit = [(me // (1 << b)) % 2 for b in range(bits)]
    peer = [me + (1 - 2 * bit[b]) * (1 << b) for b in range(bits)]
    piece = sums_ref.shape[1 + bits :]
    chunk_cols = piece[-1]

    def order_of(parity):
        order = list(range(bits))
        if parity and bits > 2:
            order[1], order[2] = order[2], order[1]
        return order

    def view(chunk, parity, phase, side):
        order = order_of(parity)
        index = []
        for b in reversed(range(bits)):
            if b in order[:phase]:
                index.append(bit[b])
            elif b == order[phase]:
                index.append(side)
            else:
                index.append(slice(None))
        return (chunk,) + tuple(index)

    def move(chunk, parity, phase):
        b = order_of(parity)[phase]
        return pltpu.make_async_remote_copy(
            src_ref=sums_ref.at[view(chunk, parity, phase, 1 - bit[b])],
            dst_ref=recv[phase].at[chunk],
            send_sem=sum_send.at[chunk, phase],
            recv_sem=sum_recv.at[chunk, phase],
            device_id={"dev": peer[b]},
            device_id_type=pl.DeviceIdType.MESH,
        )

    def finish(chunk, parity, phase):
        b = order_of(parity)[phase]
        move(chunk, parity, phase).wait_recv()
        index = view(chunk, parity, phase, bit[b])
        total = sums_ref[index].astype(full) + recv[phase][chunk].astype(full)
        if phase + 1 < bits:
            sums_ref[index] = total.astype(half)
            move(chunk, parity, phase + 1).start()
        else:
            return total.reshape(width // n, chunk_cols)

    def keep(chunk, values):
        sums_ref[chunk] = values.reshape((2,) * bits + piece).astype(half)

    outer = width // chunk_cols
    for j in range(outer):
        cols = slice(j * chunk_cols, (j + 1) * chunk_cols)
        total = 0.0
        for c in range(cohorts):
            total += dot(att_ref[c], dys_ref[c * block : (c + 1) * block, cols], ((1,), (0,)))
        keep(j, total)
        move(j, j % 2, 0).start()

    def spread_grad(b):
        at = pl.ds(pl.multiple_of(b * 2 * lanes, 2 * lanes), 2 * lanes)
        da_ref[:, at] = dot(dys_ref[...], wo_ref[at, :], ((1,), (1,))).astype(half)

    steps_to(cuts // 2, spread_grad)

    def back(g):
        at = pl.ds(pl.multiple_of(g * lanes, lanes), lanes)
        scale = scale_of(g, 1, lanes)

        def one(c):
            start = pl.multiple_of(c * block, block)
            block_rows = pl.ds(start, block)
            q, k, v = q_ref[block_rows, at], k_ref[block_rows, at], v_ref[block_rows, at]
            q_split = split(q)
            da_split = split(da_ref[block_rows, at])
            grad_probs = dot(v, da_split, ((1,), (1,)))
            probs_half = probs_ref[g * cohorts + c]
            probs = probs_half.astype(full)
            grad_v = dot(probs_half, da_split, ((1,), (0,)))
            row_dot = jnp.sum(grad_probs * probs, axis=0, keepdims=True)
            grad_scores = (probs * (grad_probs - row_dot)).astype(half)
            dk = dot(grad_scores, q_split, ((1,), (0,))) * scale
            dq = fold(dot(k.T, grad_scores, ((1,), (0,)))).T * scale
            for part, (value, unit, inv_ref) in enumerate(((dq, q, q_inv_ref), (dk, k, k_inv_ref))):
                unit = unit.astype(full)
                value = inv_ref[block_rows, at] * (value - unit * head_mean(value * unit))
                to = pl.ds(pl.multiple_of(part * width + g * lanes, lanes), lanes)
                dproj_ref[block_rows, to] = value.astype(half)
            to = pl.ds(pl.multiple_of(2 * width + g * lanes, lanes), lanes)
            dproj_ref[block_rows, to] = grad_v.astype(half)

        for c in range(cohorts):
            one(c)
        parts = [
            dproj_ref[:, pl.ds(pl.multiple_of(part * width + g * lanes, lanes), lanes)] for part in range(3)
        ]
        keep(outer + g, dot(normed_t_ref[...], jnp.concatenate(parts, axis=1), ((1,), (0,))))

    chunks = outer + groups
    turns = groups // 2

    def stage(t):
        for j in range(2):
            g = 2 * t + j
            back(g)
            move(outer + g, j, 0).start()
        for phase in reversed(range(min(bits, turns))):

            @pl.when(t >= phase)
            def _():
                for j in range(2):
                    finish(2 * (t - phase) + j, j, phase)

    steps_to(turns, stage)

    def wave(w):
        for phase in reversed(range(bits)):
            at = w - phase
            if 0 <= at < chunks // 2:
                for j in range(2):
                    chunk = 2 * at + j
                    total = finish(chunk, j, phase)
                    if phase + 1 < bits:
                        continue
                    if chunk < outer:
                        gwo_ref[:, chunk * chunk_cols : (chunk + 1) * chunk_cols] = total
                    else:
                        for part in range(3):
                            start = part * width + (chunk - outer) * lanes
                            gqkv_ref[:, start : start + lanes] = total[:, part * lanes : (part + 1) * lanes]

    def close(c):
        at = pl.ds(pl.multiple_of(c * block, block), block)
        values = xs_ref[at, :].astype(full)
        inv = lax.rsqrt(jnp.mean(values * values, axis=-1, keepdims=True) + epsilon)
        unit = values * inv
        shaped = dot(dproj_ref[at, :], wqkv_ref[...], ((1,), (1,))) * gain_ref[...]
        result = dys_ref[at, :].astype(full) + inv * (
            shaped - unit * jnp.mean(shaped * unit, axis=-1, keepdims=True)
        )
        xs_ref[at, :] = result.astype(half)

    steps_to(cohorts, close)
    sent_all(0, x_out, x_got)
    sent_all(1, dy_out, dy_got)
    quarter = n // 4

    def deliver(i):
        first_to = lax.rem(me // quarter + i, 4) * quarter
        at = pl.ds(pl.multiple_of(first_to * major, quarter * major), quarter * major)
        ends = pl.ds(pl.multiple_of(n * major + first_to * 8, quarter * 8), quarter * 8)
        body = dot(place_t_ref[at, :], xs_ref[...], ((1,), (0,)))
        tail = dot(place_t_ref[ends, :], xs_ref[...], ((1,), (0,)))
        upper = lax.broadcasted_iota(jnp.int32, (quarter * 8, middle), 0) % 8 < 4
        tail = jnp.where(upper, tail[:, 0:middle], tail[:, middle:width])
        x_out[pl.ds(first_to, quarter), 0:tiles] = (
            body[:, 0:middle].reshape(quarter, tiles, 8, middle).astype(half)
        )
        x_out[pl.ds(first_to, quarter), tiles : 2 * tiles] = (
            body[:, middle:width].reshape(quarter, tiles, 8, middle).astype(half)
        )
        x_out[pl.ds(first_to, quarter), 2 * tiles] = tail.reshape(quarter, 8, middle).astype(half)

        def launch(j):
            to = first_to + lax.rem(me + j, quarter)

            @pl.when(to != me)
            def _():
                transfer(2, x_out, gin_got, to, me).start()

        steps_to(quarter, launch)

    steps_to(4, deliver)
    gin_got[me] = x_out[me]
    for w in range(turns, chunks // 2 + bits - 1):
        wave(w)

    def put(p):
        values = gin_got[p].astype(full)
        start = pl.multiple_of(p * spread, 8)
        for b in range(cuts):
            to, at = divmod(b, cuts // 2)
            at = slice(at * lanes, (at + 1) * lanes)
            flat[b, pl.ds(start, major), :] = values[to * tiles : (to + 1) * tiles, :, at].reshape(major, lanes)
            flat[b, pl.ds(start + major, minor), :] = values[2 * tiles, to * 4 : to * 4 + minor, at]

    def land(i):
        source = before(i + 1)
        arrived(2, x_out, gin_got, source)
        put(source)

    put(me)
    steps_to(n - 1, land)

    def write(c):
        for b in range(cuts):
            gin_ref[c, :, b * lanes : (b + 1) * lanes] = flat[b, pl.ds(c, n, stride=spread), :].astype(half)

    steps_to(per, write)

    def sums_sent(chunk, parity):
        for phase in range(bits):
            move(chunk, parity, phase).wait_send()

    for j in range(2):
        steps_to(chunks // 2, lambda i: sums_sent(2 * i + j, j))
    steps_to(n - 1, lambda i: transfer(2, x_out, gin_got, other(i + 1), me).wait_send())


def fused(n, block, cohorts, hidden_in, grad_out, norm_gain, w_qkv, w_out, sharpness, cohort_ids, observed):
    per, patches, width = hidden_in.shape
    heads = sharpness.shape[0]
    head_size = width // heads
    campaigns = per * n
    lanes = 128
    rows = block * cohorts
    cuts = width // lanes
    groups = cuts
    bits = n.bit_length() - 1
    major = per - per % 16
    slots = n * (major + 8)
    chunk_cols = 3 * lanes
    chunks = width // chunk_cols + groups
    piece = (width // n // 8, 8, chunk_cols)
    half, full = jnp.bfloat16, jnp.float32
    parcel = (n, major // 4 + 1, 8, width // 2)
    anywhere = pl.BlockSpec(memory_space=pl.ANY)
    vmem = pl.BlockSpec(memory_space=pltpu.VMEM)
    scratch = [
        pltpu.VMEM((per, patches, width), half),
        pltpu.VMEM((per, patches, width), half),
        pltpu.VMEM((width, 3 * width), half),
        pltpu.VMEM((width, width), half),
        pltpu.VMEM((cuts, max(per * patches, n * (per + 8 - per % 8)), lanes), full),
    ]
    scratch += [pltpu.VMEM(parcel, half)] * 5
    scratch += [
        pltpu.VMEM((n * 8, width // 2), full),
        pltpu.VMEM((slots, width), half),
        pltpu.VMEM((rows, slots), half),
        pltpu.VMEM((slots, rows), half),
        pltpu.VMEM((rows, lanes // head_size * block), full),
        pltpu.VMEM((rows, width), half),
        pltpu.VMEM((rows, width), half),
        pltpu.VMEM((width, rows), half),
        pltpu.VMEM((rows, width), half),
        pltpu.VMEM((rows, width), half),
        pltpu.VMEM((rows, width), half),
        pltpu.VMEM((rows, width), full),
        pltpu.VMEM((rows, width), full),
        pltpu.VMEM((groups * cohorts, block, lanes // head_size * block), half),
        pltpu.VMEM((cohorts, width, block), half),
        pltpu.VMEM((rows, width), half),
        pltpu.VMEM((rows, width), half),
        pltpu.VMEM((rows, 3 * width), half),
        pltpu.VMEM((chunks,) + (2,) * bits + piece, half),
    ]
    scratch += [pltpu.VMEM((chunks,) + (2,) * (bits - 1 - p) + piece, half) for p in range(bits)]
    scratch += [
        pltpu.SemaphoreType.DMA((4,)),
        pltpu.SemaphoreType.DMA((3, n)),
        pltpu.SemaphoreType.DMA((3, n)),
        pltpu.SemaphoreType.DMA((chunks, bits)),
        pltpu.SemaphoreType.DMA((chunks, bits)),
    ]
    return pl.pallas_call(
        functools.partial(fused_kernel, n, block, cohorts, head_size),
        in_specs=[pl.BlockSpec(memory_space=pltpu.SMEM)] + [anywhere] * 4 + [vmem] * 3,
        out_specs=[vmem] * 3,
        out_shape=[
            jax.ShapeDtypeStruct((per, n, width), half),
            jax.ShapeDtypeStruct((width // n, 3 * width), full),
            jax.ShapeDtypeStruct((width // n, width), full),
        ],
        scratch_shapes=scratch,
        compiler_params=pltpu.CompilerParams(
            collective_id=1, has_side_effects=True, vmem_limit_bytes=67_043_328
        ),
        cost_estimate=pl.CostEstimate(flops=60_000_000_000, bytes_accessed=12_000_000, transcendentals=0),
    )(
        sharpness,
        hidden_in,
        grad_out,
        w_qkv,
        w_out,
        norm_gain[None, :],
        cohort_ids[None, :],
        observed.T,
    )


def fits(n, hidden_in, sharpness, observed):
    per, patches, width = hidden_in.shape
    return (
        n >= 8
        and n & (n - 1) == 0
        and patches == n
        and per % 16 == 4
        and width % (n * 8) == 0
        and width % 768 == 0
        and sharpness.shape[0] * 64 == width
        and observed.shape[1] == 1
    )


def body(n, *args):
    hidden_in, sharpness, cohort_ids, observed = args[0], args[5], args[6], args[7]
    if not fits(n, hidden_in, sharpness, observed):
        return layer(n, *args)
    block = 64 * -(-6 * hidden_in.shape[0] * n // (5 * 64 * cohort_kinds))
    kinds = jnp.arange(cohort_kinds, dtype=cohort_ids.dtype)
    most = jnp.max(jnp.sum((cohort_ids[None, :] == kinds[:, None]).astype(jnp.int32), axis=1))
    crowded = lax.pmax((most > block).astype(jnp.int32), "grp") > 0
    return lax.cond(
        crowded,
        functools.partial(layer, n),
        functools.partial(fused, n, block, cohort_kinds),
        *args,
    )


def solution(mesh):
    in_specs = (
        P(("grp", "dev"), None, None),
        P(("grp", "dev"), None, None),
        P(),
        P(),
        P(),
        P(),
        P("grp"),
        P("grp", "dev"),
    )
    out_specs = (P(("grp", "dev"), None, None), P(("grp", "dev"), None), P(("grp", "dev"), None))
    step = jax.shard_map(functools.partial(body, mesh.shape["dev"]), mesh=mesh, in_specs=in_specs, out_specs=out_specs, check_vma=False)
    return step
```

profile of v0, /device:TPU:0, one launch (start us, length us, event | category | flops | bytes accessed | tf_op | source)
XLA Modules:
  0.0 142.4 jit_solution(17556188743912131210)
XLA Ops:
  0.6 0.8 convert_reduce_fusion
  1.4 0.6 reduce_max.9
  2.7 136.1 %conditional.1 = (f32[24,2304]{1,0:T(8,128)}, f32[24,768]{1,0:T(8,128)}, bf16[20,32,768]{2,1,0:T(8,128)(2,1)}) conditional(s32[]{:T(128)} %convert_element_type.11, (f32[768]{0:T(1024)}, s32[640]{0:T(1024)}, s32[640,1]{0,1:T(1,128)}, f32[12]{0:T(128)}, bf16[20,32,768]{2,1,0:T(8,128)(2,1)}, /*index=5*/bf16[20,32,768]{2,1,0:T(8,128)(2,1)}, ...), branch_computations={%region_2.0_spmd, %region_3.0_spmd} | conditional | flops 112999989248 | bytes 107206224 | solution.py:1000
  2.7 1.3 broadcast_in_dim.1.cohort_ref
  4.0 1.3 broadcast_in_dim.0.gain_ref
  5.3 133.1 %branch_0_fun.1 = (bf16[20,32,768]{2,1,0:T(8,128)(2,1)}, f32[24,2304]{1,0:T(8,128)}, f32[24,768]{1,0:T(8,128)}) custom-call(f32[12]{0:T(128)} %get-tuple-element.32.sharp_ref, bf16[20,32,768]{2,1,0:T(8,128)(2,1)} %get-tuple-element.33.x_hbm, bf16[20,32,768]{2,1,0:T(8,128)(2,1)} %get-tuple-element.34.dy_hbm, bf16[768,2304]{1,0:T(8,128)(2,1)} %get-tuple-element.35.wqkv_hbm, ...), custom_call_target="tpu_custom_call" | custom-call | flops 60000002048 | bytes 12000000 | tf_op jit(solution)/shard_map/cond/branch_0_fun/pallas_call | solution.py:952
  138.8 0.0 copy-start.6
  138.9 0.0 copy-start.7
  138.9 2.3 %copy.60 = bf16[20,32,768]{2,1,0:T(8,128)(2,1)} copy(bf16[20,32,768]{2,1,0:T(8,128)(2,1)} %get-tuple-element.123) | data formatting | bytes 1966080
  141.1 0.0 copy-done.6
  141.1 0.7 copy.61
  141.8 0.0 copy-done.7
  141.8 0.6 copy.62
Async XLA Ops:
  138.8 2.3 %copy-start.6 = (f32[24,2304]{1,0:T(8,128)S(1)}, f32[24,2304]{1,0:T(8,128)}, u32[]{:S(2)}) copy-start(f32[24,2304]{1,0:T(8,128)} %get-tuple-element.124) | copy-start | bytes 663556
  138.9 3.0 %copy-start.7 = (f32[24,768]{1,0:T(8,128)S(1)}, f32[24,768]{1,0:T(8,128)}, u32[]{:S(2)}) copy-start(f32[24,768]{1,0:T(8,128)} %get-tuple-element.125) | copy-start | bytes 221188
where the time goes:
time: 143 us; the launch traced here: 142 us
  Pallas kernels  133 us (93%)
  local copies, waits for them, and re-layouts  6.11 us (4%)
  other arithmetic  1.44 us (1%)
    pallas_call x1, Pallas kernels, fused(): pl.pallas_call(functools.partial(fused_kernel, n, block, cohorts, head_si...  133 us
    unnamed x7, local copies, waits for them, and re-layouts  3.58 us

commit v1 on v0

--- a/solution.py
+++ b/solution.py
@@ -441,6 +441,7 @@
     dys_ref,
     da_ref,
     dproj_ref,
+    ones_ref,
     sums_ref,
     *rest,
 ):
@@ -455,14 +456,14 @@
     middle = width // 2
     rows = block * cohorts
     heads = width // head_size
+    quad = 2 * lanes
     pair = lanes // head_size
-    groups = heads // pair
-    wide = pair * block
+    groups = width // quad
+    wide = 2 * pair * block
     major = per - per % 16
     minor = per % 16
     tiles = major // 8
     spread = per + 8 - per % 8
-    log_heads = groups
     me = lax.axis_index("dev")
 
     def other(i):
@@ -537,7 +538,7 @@
     dy_got[me] = dy_out[me]
     send_all(1, dy_out, dy_got)
 
-    cohort = cohort_ref[...]
+    cohort = cohort_ref[...].reshape(1, campaigns)
     line8 = jnp.broadcast_to(cohort.astype(full), (8, campaigns))
     column = line8.T[:, 0:1]
     same = (column == cohort.astype(full)) & (
@@ -576,19 +577,18 @@
         square = jnp.where((row == col) | (mine > 0.5), 1.0, 0.0)
         mask_ref[c * block : (c + 1) * block, :] = jnp.concatenate([square] * pair, axis=1)
 
-    lane = lax.broadcasted_iota(jnp.int32, (1, lanes), 1)
-    ones_row = lax.broadcasted_iota(jnp.int32, (2 * lanes, lanes), 0) % lanes // head_size
-    ones_col = lax.broadcasted_iota(jnp.int32, (2 * lanes, lanes), 1) // head_size
-    ones = jnp.where(ones_row == ones_col, 1.0 / head_size, 0.0).astype(half)
+    lane = lax.broadcasted_iota(jnp.int32, (1, quad), 1) // head_size
+
+    ones_row = lax.broadcasted_iota(jnp.int32, (quad, quad), 0) // head_size
+    ones_col = lax.broadcasted_iota(jnp.int32, (quad, quad), 1) // head_size
+    ones_ref[...] = jnp.where(ones_row == ones_col, 1.0 / head_size, 0.0).astype(half)
 
     def head_mean(values):
-        upper = values.astype(half)
-        lower = (values - upper.astype(full)).astype(half)
-        return dot(jnp.concatenate([upper, lower], axis=1), ones, ((1,), (0,)))
+        return dot(values.astype(half), ones_ref[...], ((1,), (0,)))
 
     def split(values):
         return jnp.concatenate(
-            [jnp.where(lane // head_size == h, values, jnp.zeros_like(values)) for h in range(pair)], axis=0
+            [jnp.where(lane == h, values, jnp.zeros_like(values)) for h in range(2 * pair)], axis=0
         )
 
     def gather(kind, out, got):
@@ -623,7 +623,7 @@
         values = dot(place_ref[at, :], got_ref[...], ((1,), (0,)))
         xs_ref[at, :] = values.astype(half)
         inv = lax.rsqrt(jnp.mean(values * values, axis=-1, keepdims=True) + epsilon)
-        normed_ref[at, :] = (values * inv * gain_ref[...]).astype(half)
+        normed_ref[at, :] = (values * inv * gain_ref[...].reshape(1, width)).astype(half)
 
     steps_to(cohorts, settle)
 
@@ -631,50 +631,51 @@
         at = pl.ds(pl.multiple_of(b * lanes, lanes), lanes)
         normed_t_ref[at, :] = normed_ref[:, at].astype(full).T.astype(half)
 
+    def quad_at(g, part=0):
+        return pl.ds(pl.multiple_of(part * width + g * quad, quad), quad)
+
     def project(g):
-        def raw(part):
-            at = pl.ds(pl.multiple_of(part * width + g * lanes, lanes), lanes)
-            return dot(normed_ref[...], wqkv_ref[:, at], ((1,), (0,)))
-
-        at = pl.ds(pl.multiple_of(g * lanes, lanes), lanes)
+        at = quad_at(g)
         for part, (unit_ref, inv_ref) in enumerate(((q_ref, q_inv_ref), (k_ref, k_inv_ref))):
-            values = raw(part)
+            values = dot(normed_ref[...], wqkv_ref[:, quad_at(g, part)], ((1,), (0,)))
             inv = lax.rsqrt(head_mean(values * values) + epsilon)
             unit_ref[:, at] = (values * inv).astype(half)
             inv_ref[:, at] = inv
-        v_ref[:, at] = raw(2).astype(half)
+        v_ref[:, at] = dot(normed_ref[...], wqkv_ref[:, quad_at(g, 2)], ((1,), (0,))).astype(half)
 
     steps_to(groups, project)
     steps_to(cuts, turn)
 
-    def scale_of(g, axis, size):
-        shape = (1, size) if axis else (size, 1)
-        index = lax.broadcasted_iota(jnp.int32, shape, axis)
-        scale = jnp.zeros(shape, full)
-        for h in range(pair):
-            scale = jnp.where(index // (size // pair) == h, sharp_ref[g * pair + h] / head_size, scale)
+    def scale_of(g, each):
+        index = lax.broadcasted_iota(jnp.int32, (1, 2 * pair * each), 1) // each
+        scale = jnp.zeros(index.shape, full)
+        for h in range(2 * pair):
+            scale = jnp.where(index == h, sharp_ref[g * 2 * pair + h] / head_size, scale)
         return scale
 
-    def fold(values):
-        return jnp.concatenate(
-            [
-                values[h * head_size : (h + 1) * head_size, h * block : (h + 1) * block]
-                for h in range(pair)
-            ],
-            axis=0,
-        )
+    def crossed(left, right):
+        rows_of = []
+        for i in range(2):
+            values = dot(
+                left[i * lanes : (i + 1) * lanes],
+                right[:, i * pair * block : (i + 1) * pair * block],
+                ((1,), (0,)),
+            )
+            for h in range(pair):
+                rows_of.append(values[h * head_size : (h + 1) * head_size, h * block : (h + 1) * block])
+        return jnp.concatenate(rows_of, axis=0)
 
     def attend(g):
-        at = pl.ds(pl.multiple_of(g * lanes, lanes), lanes)
-        scale = scale_of(g, 1, wide) * log2e
+        at = quad_at(g)
+        scale = scale_of(g, block) * log2e
         for c in range(cohorts):
             block_rows = slice(c * block, (c + 1) * block)
             scores = dot(k_ref[block_rows, at], split(q_ref[block_rows, at]), ((1,), (1,)))
-            weights = jnp.exp2(scores * scale) * mask_ref[block_rows, :]
+            mask = mask_ref[block_rows, :]
+            weights = jnp.exp2(scores * scale) * jnp.concatenate([mask, mask], axis=1)
             probs = (weights * (1.0 / jnp.sum(weights, axis=0, keepdims=True))).astype(half)
             probs_ref[g * cohorts + c] = probs
-            att = dot(v_ref[block_rows, at].T, probs, ((1,), (0,)))
-            att_ref[c, at, :] = fold(att).astype(half)
+            att_ref[c, at, :] = crossed(v_ref[block_rows, at].T, probs).astype(half)
 
     steps_to(groups, attend)
 
@@ -731,17 +732,21 @@
         else:
             return total.reshape(width // n, chunk_cols)
 
-    def keep(chunk, values):
-        sums_ref[chunk] = values.reshape((2,) * bits + piece).astype(half)
-
-    outer = width // chunk_cols
-    for j in range(outer):
-        cols = slice(j * chunk_cols, (j + 1) * chunk_cols)
-        total = 0.0
-        for c in range(cohorts):
-            total += dot(att_ref[c], dys_ref[c * block : (c + 1) * block, cols], ((1,), (0,)))
-        keep(j, total)
-        move(j, j % 2, 0).start()
+    def keep(first_chunk, values):
+        for j in range(2):
+            part = values[:, j * chunk_cols : (j + 1) * chunk_cols]
+            sums_ref[first_chunk + j] = part.reshape((2,) * bits + piece).astype(half)
+        for j in range(2):
+            move(first_chunk + j, j, 0).start()
+
+    def finish_pair(at, phase):
+        for j in range(2):
+            finish(2 * at + j, j, phase)
+
+    total = 0.0
+    for c in range(cohorts):
+        total += dot(att_ref[c], dys_ref[c * block : (c + 1) * block, :], ((1,), (0,)))
+    keep(0, total)
 
     def spread_grad(b):
         at = pl.ds(pl.multiple_of(b * 2 * lanes, 2 * lanes), 2 * lanes)
@@ -749,13 +754,26 @@
 
     steps_to(cuts // 2, spread_grad)
 
+    def settle_sums(at, phase):
+        for j in range(2):
+            chunk = 2 * at + j
+            total = finish(chunk, j, phase)
+            if phase + 1 < bits:
+                continue
+            for i in range(chunk_cols // lanes):
+                values = total[:, i * lanes : (i + 1) * lanes]
+                spot = j * (chunk_cols // lanes) + i
+                if at == 0:
+                    gwo_ref[:, spot * lanes : (spot + 1) * lanes] = values
+                else:
+                    start = spot // 2 * width + (at - 1) * quad + spot % 2 * lanes
+                    gqkv_ref[:, start : start + lanes] = values
+
     def back(g):
-        at = pl.ds(pl.multiple_of(g * lanes, lanes), lanes)
-        scale = scale_of(g, 1, lanes)
-
-        def one(c):
-            start = pl.multiple_of(c * block, block)
-            block_rows = pl.ds(start, block)
+        at = quad_at(g)
+        scale = scale_of(g, head_size)
+        for c in range(cohorts):
+            block_rows = slice(c * block, (c + 1) * block)
             q, k, v = q_ref[block_rows, at], k_ref[block_rows, at], v_ref[block_rows, at]
             q_split = split(q)
             da_split = split(da_ref[block_rows, at])
@@ -766,67 +784,45 @@
             row_dot = jnp.sum(grad_probs * probs, axis=0, keepdims=True)
             grad_scores = (probs * (grad_probs - row_dot)).astype(half)
             dk = dot(grad_scores, q_split, ((1,), (0,))) * scale
-            dq = fold(dot(k.T, grad_scores, ((1,), (0,)))).T * scale
+            dq = crossed(k.T, grad_scores).T * scale
             for part, (value, unit, inv_ref) in enumerate(((dq, q, q_inv_ref), (dk, k, k_inv_ref))):
                 unit = unit.astype(full)
                 value = inv_ref[block_rows, at] * (value - unit * head_mean(value * unit))
-                to = pl.ds(pl.multiple_of(part * width + g * lanes, lanes), lanes)
-                dproj_ref[block_rows, to] = value.astype(half)
-            to = pl.ds(pl.multiple_of(2 * width + g * lanes, lanes), lanes)
-            dproj_ref[block_rows, to] = grad_v.astype(half)
-
-        for c in range(cohorts):
-            one(c)
-        parts = [
-            dproj_ref[:, pl.ds(pl.multiple_of(part * width + g * lanes, lanes), lanes)] for part in range(3)
-        ]
-        keep(outer + g, dot(normed_t_ref[...], jnp.concatenate(parts, axis=1), ((1,), (0,))))
-
-    chunks = outer + groups
-    turns = groups // 2
-
-    def stage(t):
-        for j in range(2):
-            g = 2 * t + j
-            back(g)
-            move(outer + g, j, 0).start()
-        for phase in reversed(range(min(bits, turns))):
-
-            @pl.when(t >= phase)
-            def _():
-                for j in range(2):
-                    finish(2 * (t - phase) + j, j, phase)
-
-    steps_to(turns, stage)
-
-    def wave(w):
-        for phase in reversed(range(bits)):
-            at = w - phase
-            if 0 <= at < chunks // 2:
-                for j in range(2):
-                    chunk = 2 * at + j
-                    total = finish(chunk, j, phase)
-                    if phase + 1 < bits:
-                        continue
-                    if chunk < outer:
-                        gwo_ref[:, chunk * chunk_cols : (chunk + 1) * chunk_cols] = total
-                    else:
-                        for part in range(3):
-                            start = part * width + (chunk - outer) * lanes
-                            gqkv_ref[:, start : start + lanes] = total[:, part * lanes : (part + 1) * lanes]
+                dproj_ref[block_rows, quad_at(g, part)] = value.astype(half)
+            dproj_ref[block_rows, quad_at(g, 2)] = grad_v.astype(half)
+            for phase, lag, when in progress:
+                if when == c and lag < groups:
+
+                    @pl.when(g >= lag)
+                    def _():
+                        finish_pair(g - lag, phase)
+
+        parts = [dproj_ref[:, quad_at(g, part)] for part in range(3)]
+        keep(2 * g + 2, dot(normed_t_ref[...], jnp.concatenate(parts, axis=1), ((1,), (0,))))
+
+    last = cohorts - 1
+    progress = [(phase, phase, last) for phase in reversed(range(bits))]
+    steps_to(groups, back)
+    pairs = groups + 1
+
+    def advance(turn, c):
+        for phase, lag, when in progress:
+            if when == c and 0 <= turn - lag < pairs:
+                settle_sums(turn - lag, phase)
 
     def close(c):
         at = pl.ds(pl.multiple_of(c * block, block), block)
         values = xs_ref[at, :].astype(full)
         inv = lax.rsqrt(jnp.mean(values * values, axis=-1, keepdims=True) + epsilon)
         unit = values * inv
-        shaped = dot(dproj_ref[at, :], wqkv_ref[...], ((1,), (1,))) * gain_ref[...]
+        shaped = dot(dproj_ref[at, :], wqkv_ref[...], ((1,), (1,))) * gain_ref[...].reshape(1, width)
         result = dys_ref[at, :].astype(full) + inv * (
             shaped - unit * jnp.mean(shaped * unit, axis=-1, keepdims=True)
         )
         xs_ref[at, :] = result.astype(half)
 
-    steps_to(cohorts, close)
+    for c in range(cohorts):
+        close(c)
     sent_all(0, x_out, x_got)
     sent_all(1, dy_out, dy_got)
     quarter = n // 4
@@ -858,8 +854,9 @@
 
     steps_to(4, deliver)
     gin_got[me] = x_out[me]
-    for w in range(turns, chunks // 2 + bits - 1):
-        wave(w)
+    for turn in range(groups, pairs + bits):
+        for c in range(cohorts):
+            advance(turn, c)
 
     def put(p):
         values = gin_got[p].astype(full)
@@ -889,7 +886,7 @@
             move(chunk, parity, phase).wait_send()
 
     for j in range(2):
-        steps_to(chunks // 2, lambda i: sums_sent(2 * i + j, j))
+        steps_to(pairs, lambda i: sums_sent(2 * i + j, j))
     steps_to(n - 1, lambda i: transfer(2, x_out, gin_got, other(i + 1), me).wait_send())
 
 
@@ -901,12 +898,12 @@
     lanes = 128
     rows = block * cohorts
     cuts = width // lanes
-    groups = cuts
+    groups = cuts // 2
     bits = n.bit_length() - 1
     major = per - per % 16
     slots = n * (major + 8)
     chunk_cols = 3 * lanes
-    chunks = width // chunk_cols + groups
+    chunks = 2 + 2 * groups
     piece = (width // n // 8, 8, chunk_cols)
     half, full = jnp.bfloat16, jnp.float32
     parcel = (n, major // 4 + 1, 8, width // 2)
@@ -934,11 +931,12 @@
         pltpu.VMEM((rows, width), half),
         pltpu.VMEM((rows, width), full),
         pltpu.VMEM((rows, width), full),
-        pltpu.VMEM((groups * cohorts, block, lanes // head_size * block), half),
+        pltpu.VMEM((groups * cohorts, block, 2 * lanes // head_size * block), half),
         pltpu.VMEM((cohorts, width, block), half),
         pltpu.VMEM((rows, width), half),
         pltpu.VMEM((rows, width), half),
         pltpu.VMEM((rows, 3 * width), half),
+        pltpu.VMEM((2 * lanes, 2 * lanes), half),
         pltpu.VMEM((chunks,) + (2,) * bits + piece, half),
     ]
     scratch += [pltpu.VMEM((chunks,) + (2,) * (bits - 1 - p) + piece, half) for p in range(bits)]
@@ -969,8 +967,8 @@
         grad_out,
         w_qkv,
         w_out,
-        norm_gain[None, :],
-        cohort_ids[None, :],
+        norm_gain,
+        cohort_ids,
         observed.T,
     )
 
@@ -986,6 +984,7 @@
         and width % 768 == 0
         and sharpness.shape[0] * 64 == width
         and observed.shape[1] == 1
+        and width // 256 < n.bit_length() - 1
     )
 
 

time: 143 us -> 131 us (0.916)
  Pallas kernels: 133 us -> 124 us
  local copies, waits for them, and re-layouts: 6.11 us -> 3.58 us
    pallas_call x1, Pallas kernels: 133 us -> 124 us  [fused(): pl.pallas_call(functools.partial(fused_kernel, n, block, cohorts, head_si...]
    broadcast_in_dim x2 -> x0, local copies, waits for them, and re-layouts: 2.54 us -> none  [the longest x1 1.27 us: fused(): cohort_ids[None, :]]
where the time goes in v1:
time: 131 us; the launch traced here: 130 us
  Pallas kernels  124 us (95%)
  local copies, waits for them, and re-layouts  3.58 us (3%)
  other arithmetic  1.44 us (1%)
  between operations  1.31 us (1%)
    pallas_call x1, Pallas kernels, fused(): pl.pallas_call(functools.partial(fused_kernel, n, block, cohorts, head_si...  124 us
    unnamed x7, local copies, waits for them, and re-layouts  3.58 us

profile of v1, /device:TPU:0, one launch (start us, length us, event | category | flops | bytes accessed | tf_op | source)
XLA Modules:
  0.0 130.4 jit_solution(11118447999038285260)
XLA Ops:
  0.6 0.8 convert_reduce_fusion
  1.4 0.6 reduce_max.9
  2.7 124.1 %conditional.1 = (f32[24,2304]{1,0:T(8,128)}, f32[24,768]{1,0:T(8,128)}, bf16[20,32,768]{2,1,0:T(8,128)(2,1)}) conditional(s32[]{:T(128)} %convert_element_type.11, (s32[640,1]{0,1:T(1,128)}, f32[12]{0:T(128)}, bf16[20,32,768]{2,1,0:T(8,128)(2,1)}, bf16[20,32,768]{2,1,0:T(8,128)(2,1)}, bf16[768,2304]{1,0:T(8,128)(2,1)}, ...), branch_computations={%region_2.0_spmd, %region_3.0_spmd} | conditional | flops 112999989248 | bytes 107206224 | solution.py:999
  2.7 123.6 %branch_0_fun.1 = (bf16[20,32,768]{2,1,0:T(8,128)(2,1)}, f32[24,2304]{1,0:T(8,128)}, f32[24,768]{1,0:T(8,128)}) custom-call(f32[12]{0:T(128)} %get-tuple-element.32.sharp_ref, bf16[20,32,768]{2,1,0:T(8,128)(2,1)} %get-tuple-element.33.x_hbm, bf16[20,32,768]{2,1,0:T(8,128)(2,1)} %get-tuple-element.34.dy_hbm, bf16[768,2304]{1,0:T(8,128)(2,1)} %get-tuple-element.35.wqkv_hbm, ...), custom_call_target="tpu_custom_call" | custom-call | flops 60000002048 | bytes 12000000 | tf_op jit(solution)/shard_map/cond/branch_0_fun/pallas_call | solution.py:950
  126.8 0.0 copy-start.6
  126.9 0.0 copy-start.7
  126.9 2.3 %copy.60 = bf16[20,32,768]{2,1,0:T(8,128)(2,1)} copy(bf16[20,32,768]{2,1,0:T(8,128)(2,1)} %get-tuple-element.123) | data formatting | bytes 1966080
  129.1 0.0 copy-done.6
  129.1 0.7 copy.61
  129.8 0.0 copy-done.7
  129.8 0.6 copy.62
Async XLA Ops:
  126.8 2.3 %copy-start.6 = (f32[24,2304]{1,0:T(8,128)S(1)}, f32[24,2304]{1,0:T(8,128)}, u32[]{:S(2)}) copy-start(f32[24,2304]{1,0:T(8,128)} %get-tuple-element.124) | copy-start | bytes 663556
  126.9 3.0 %copy-start.7 = (f32[24,768]{1,0:T(8,128)S(1)}, f32[24,768]{1,0:T(8,128)}, u32[]{:S(2)}) copy-start(f32[24,768]{1,0:T(8,128)} %get-tuple-element.125) | copy-start | bytes 221188
